TPU v7x, 128 devices: a whole 4x4x4 slice. The times are simulated.
128 devices in a mesh: blk: 32 (over z_lo, y, x), head: 4 (over z_hi, core).
Axes of the slice: x: 4, y: 4, z: 4 (z_hi: 2, z_lo: 2; z = z_hi * 2 + z_lo), core: 2. Of those that a mesh axis runs over, the one named last changes fastest.
Arguments:
- query_vectors: bfloat16 [4096, 2560], P('blk', 'head'), may hold values from -8 to 8
- key_vectors: bfloat16 [4096, 2560], P('blk', 'head'), may hold values from -8 to 8, as said below
- value_vectors: bfloat16 [4096, 2560], P('blk', 'head'), may hold values from -6 to 6
- tangent_queries: bfloat16 [4096, 2560], P('blk', 'head'), may hold values from -6 to 6
- tangent_keys: bfloat16 [4096, 2560], P('blk', 'head'), may hold values from -6 to 6
- tangent_values: bfloat16 [4096, 2560], P('blk', 'head'), may hold values from -6 to 6
- target_gap: bfloat16 [4096, 2560], P(('blk', 'head')), may hold values from -6 to 6
Outputs:
- primal_out: bfloat16 [4096, 2560], P(('blk', 'head'))
- tangent_out: bfloat16 [4096, 2560], P(('blk', 'head'))
- query_grad: bfloat16 [4096, 2560], P('blk', 'head')
- key_grad: bfloat16 [4096, 2560], P('blk', 'head')
- value_grad: bfloat16 [4096, 2560], P('blk', 'head')
Inputs may be any that keep to these rules, and one draw needn't show every extreme that they name: `key_vectors`: keys are real-valued draws.
All inputs are finite; a program needn't handle non-finite values.
Results may differ from a plain program's by a relative error of at most 0.015.
Values may be sent and summed in bfloat16 or wider, within the bound.
No kernel may reach another device: no remote copies, remote signals or barrier semaphores. Data moves between devices by JAX's collectives and lax.ppermute only.
A program may use at most 128 MiB of HBM per device.

v0:
```python
from functools import partial
import math
import jax
import jax.numpy as jnp
from jax import lax
from jax.sharding import PartitionSpec as P

HD = 128
scale_loss = 64.0
floor_value = -1e30


def split_heads(matrix, head_count):
    return matrix.reshape(matrix.shape[0], head_count, matrix.shape[1] // head_count)


def fold_blocks(advance, running, operands, length):
    block_rows = length
    while block_rows > 512 and block_rows % 2 == 0:
        block_rows = block_rows // 2
    block_total = length // block_rows

    def one_block(position, carried):
        slices = tuple(
            (
                lax.dynamic_slice_in_dim(member, position * block_rows, block_rows, 0)
                for member in operands
            )
        )
        return advance(carried, slices)

    return lax.fori_loop(0, block_total, one_block, running)


def forward_update(nearby, running, slices):
    near_queries, near_tangents, inverse = nearby
    far_keys, far_values, far_tan_keys, far_tan_values = slices
    row_peak, denominator, tan_weight, primal_sum, tangent_sum = running
    scores = (
        jnp.einsum("qhd,khd->qhk", near_queries, far_keys, preferred_element_type=jnp.float32)
        * inverse
    )
    tan_scores = (
        jnp.einsum("qhd,khd->qhk", near_tangents, far_keys, preferred_element_type=jnp.float32)
        + jnp.einsum("qhd,khd->qhk", near_queries, far_tan_keys, preferred_element_type=jnp.float32)
    ) * inverse
    new_peak = jnp.maximum(row_peak, jnp.max(scores, axis=2))
    factor = jnp.exp(row_peak - new_peak)
    weights = jnp.exp(scores - new_peak[:, :, None])
    weighted_tan = weights * tan_scores
    denominator = factor * denominator + jnp.sum(weights, axis=2)
    tan_weight = factor * tan_weight + jnp.sum(weighted_tan, axis=2)
    weights_low = weights.astype(jnp.bfloat16)
    tan_low = weighted_tan.astype(jnp.bfloat16)
    primal_sum = factor[:, :, None] * primal_sum + jnp.einsum(
        "qhk,khd->qhd", weights_low, far_values, preferred_element_type=jnp.float32
    )
    tangent_sum = (
        factor[:, :, None] * tangent_sum
        + jnp.einsum("qhk,khd->qhd", tan_low, far_values, preferred_element_type=jnp.float32)
        + jnp.einsum(
            "qhk,khd->qhd", weights_low, far_tan_values, preferred_element_type=jnp.float32
        )
    )
    return (new_peak, denominator, tan_weight, primal_sum, tangent_sum)


def query_update(nearby, running, slices):
    near_queries, near_cotangent, log_total, inner_sums, inverse = nearby
    far_keys, far_values = slices
    scores = (
        jnp.einsum("qhd,khd->qhk", near_queries, far_keys, preferred_element_type=jnp.float32)
        * inverse
    )
    chances = jnp.exp(scores - log_total[:, :, None])
    prob_grad = jnp.einsum(
        "qhd,khd->qhk", near_cotangent, far_values, preferred_element_type=jnp.float32
    )
    score_grad = (chances * (prob_grad - inner_sums[:, :, None])).astype(jnp.bfloat16)
    return running + jnp.einsum(
        "qhk,khd->qhd", score_grad, far_keys, preferred_element_type=jnp.float32
    )


def key_update(nearby, running, slices):
    near_keys, near_values, inverse = nearby
    far_queries, far_cotangent, far_log, far_inner = slices
    key_acc, value_acc = running
    scores = (
        jnp.einsum("qhd,khd->qhk", far_queries, near_keys, preferred_element_type=jnp.float32)
        * inverse
    )
    chances = jnp.exp(scores - far_log[:, :, None])
    value_acc = value_acc + jnp.einsum(
        "qhk,qhd->khd",
        chances.astype(jnp.bfloat16),
        far_cotangent,
        preferred_element_type=jnp.float32,
    )
    prob_grad = jnp.einsum(
        "qhd,khd->qhk", far_cotangent, near_values, preferred_element_type=jnp.float32
    )
    score_grad = (chances * (prob_grad - far_inner[:, :, None])).astype(jnp.bfloat16)
    key_acc = key_acc + jnp.einsum(
        "qhk,qhd->khd", score_grad, far_queries, preferred_element_type=jnp.float32
    )
    return (key_acc, value_acc)


def per_device(
    query_vectors,
    key_vectors,
    value_vectors,
    tangent_queries,
    tangent_keys,
    tangent_values,
    target_gap,
):
    local_rows = query_vectors.shape[0]
    local_feat = query_vectors.shape[1]
    head_count = local_feat // HD
    inverse = 1.0 / math.sqrt(HD)
    near_queries = split_heads(query_vectors, head_count)
    near_tangents = split_heads(tangent_queries, head_count)
    near_keys = split_heads(key_vectors, head_count)
    near_values = split_heads(value_vectors, head_count)
    row_zeros = jnp.zeros((local_rows, head_count), jnp.float32)
    sum_zeros = jnp.zeros((local_rows, head_count, HD), jnp.float32)
    stats_start = (
        jnp.full((local_rows, head_count), floor_value, jnp.float32),
        row_zeros,
        row_zeros,
        sum_zeros,
        sum_zeros,
    )
    extra_start = ()
    shards = (
        lax.all_gather(key_vectors, "blk", axis=0, tiled=True),
        lax.all_gather(value_vectors, "blk", axis=0, tiled=True),
        lax.all_gather(tangent_keys, "blk", axis=0, tiled=True),
        lax.all_gather(tangent_values, "blk", axis=0, tiled=True),
    )
    stats = stats_start
    extras = extra_start
    operands = tuple((split_heads(member, head_count) for member in shards))
    stats = fold_blocks(
        partial(forward_update, (near_queries, near_tangents, inverse)),
        stats,
        operands,
        shards[0].shape[0],
    )
    stats, extras = (stats, extras)
    row_peak, denominator, tan_weight, primal_sum, tangent_sum = stats
    primal = primal_sum / denominator[:, :, None]
    tangent = (
        tangent_sum / denominator[:, :, None] - (tan_weight / denominator)[:, :, None] * primal
    )
    primal_low = primal.astype(jnp.bfloat16)
    tangent_low = tangent.astype(jnp.bfloat16).reshape(local_rows, -1)
    primal_out, tangent_out = (
        lax.all_to_all(
            primal_low.reshape(local_rows, -1), "head", split_axis=0, concat_axis=1, tiled=True
        ),
        lax.all_to_all(tangent_low, "head", split_axis=0, concat_axis=1, tiled=True),
    )
    token_cotangent = (
        scale_loss * (target_gap.astype(jnp.float32) + tangent_out.astype(jnp.float32))
    ).astype(jnp.bfloat16)
    cotangent = lax.all_to_all(token_cotangent, "head", split_axis=1, concat_axis=0, tiled=True)
    near_cotangent = split_heads(cotangent, head_count)
    log_total = row_peak + jnp.log(denominator)
    inner_sums = jnp.sum(
        near_cotangent.astype(jnp.float32) * primal_low.astype(jnp.float32), axis=2
    )
    all_log, all_inner = (
        lax.all_gather(log_total, "blk", axis=0, tiled=True),
        lax.all_gather(inner_sums, "blk", axis=0, tiled=True),
    )
    query_nearby = (near_queries, near_cotangent, log_total, inner_sums, inverse)
    key_nearby = (near_keys, near_values, inverse)
    shards = (
        lax.all_gather(key_vectors, "blk", axis=0, tiled=True),
        lax.all_gather(value_vectors, "blk", axis=0, tiled=True),
        lax.all_gather(query_vectors, "blk", axis=0, tiled=True),
        lax.all_gather(cotangent, "blk", axis=0, tiled=True),
    )
    query_acc = sum_zeros
    key_acc = sum_zeros
    value_acc = sum_zeros
    length = shards[0].shape[0]
    far_keys, far_values, far_queries, far_cotangent = tuple(
        (split_heads(member, head_count) for member in shards)
    )
    query_acc = fold_blocks(
        partial(query_update, query_nearby), query_acc, (far_keys, far_values), length
    )
    key_acc, value_acc = fold_blocks(
        partial(key_update, key_nearby),
        (key_acc, value_acc),
        (far_queries, far_cotangent, all_log, all_inner),
        length,
    )
    query_acc, key_acc, value_acc = (query_acc, key_acc, value_acc)
    query_grad = (query_acc * inverse).astype(jnp.bfloat16).reshape(local_rows, -1)
    key_grad = (key_acc * inverse).astype(jnp.bfloat16).reshape(local_rows, -1)
    value_grad = value_acc.astype(jnp.bfloat16).reshape(local_rows, -1)
    return (primal_out, tangent_out, query_grad, key_grad, value_grad)


def solution(mesh):
    return jax.shard_map(
        per_device,
        mesh=mesh,
        in_specs=(
            P("blk", "head"),
            P("blk", "head"),
            P("blk", "head"),
            P("blk", "head"),
            P("blk", "head"),
            P("blk", "head"),
            P(("blk", "head"), None),
        ),
        out_specs=(
            P(("blk", "head"), None),
            P(("blk", "head"), None),
            P("blk", "head"),
            P("blk", "head"),
            P("blk", "head"),
        ),
        check_vma=False,
    )
```

profile of v0, /device:TPU:78, one launch (start us, length us, event | category | flops | bytes accessed | tf_op | source)
XLA Modules:
  0.0 1064.1 jit_solution(17173733373195373709)
XLA Ops:
  14.2 140.8 %all-gather.7.cloned.1.call-done = bf16[4096,640]{0,1:T(8,128)(2,1)} async-done(((bf16[128,640]{0,1:T(8,128)(2,1)}), bf16[4096,640]{0,1:T(8,128)(2,1)}) %all-gather.7.cloned.1.call-update) | async-done | bytes 5242896 | tf_op jit(solution)/shard_map/all_gather | solution.py:138
  155.0 7.9 copy.151
  162.8 143.4 %all-gather.13.cloned.1.call-done = bf16[4096,640]{1,0:T(8,128)(2,1)} async-done(((bf16[128,640]{1,0:T(8,128)(2,1)}), bf16[4096,640]{1,0:T(8,128)(2,1)}) %all-gather.13.cloned.1.call-update) | async-done | bytes 5242896 | tf_op jit(solution)/shard_map/all_gather | solution.py:141
  306.3 8.0 copy.150
  314.2 148.9 %all-gather.11.cloned.1.call-done = bf16[4096,640]{0,1:T(8,128)(2,1)} async-done(((bf16[128,640]{0,1:T(8,128)(2,1)}), bf16[4096,640]{0,1:T(8,128)(2,1)}) %all-gather.11.cloned.1.call-update) | async-done | bytes 5242896 | tf_op jit(solution)/shard_map/all_gather | solution.py:139
  463.1 146.8 %all-gather.9.cloned.1.call-done = bf16[4096,640]{0,1:T(8,128)(2,1)} async-done(((bf16[128,640]{0,1:T(8,128)(2,1)}), bf16[4096,640]{0,1:T(8,128)(2,1)}) %all-gather.9.cloned.1.call-update) | async-done | bytes 5242896 | tf_op jit(solution)/shard_map/all_gather | solution.py:140
  609.9 73.8 %while.52 = (s32[]{:T(128)}, f32[128,5]{0,1:T(8,128)S(1)}, f32[128,5]{0,1:T(8,128)S(1)}, f32[128,5]{0,1:T(8,128)S(1)}, f32[128,5,128]{0,2,1:T(8,128)S(1)}, /*ind...) while((s32[]{:T(128)}, f32[128,5]{0,1:T(8,128)S(1)}, ...), condition=%wide.region_4.0_spmd.clone, body=%wide.region_0.0_spmd.clone.sunk | while | flops 508481920 | bytes 16937192 | solution.py:32
  685.0 8.1 all_to_all.57
  693.2 9.5 all_to_all.58
  703.7 63.6 %all_gather.31 = f32[4096,5]{0,1:T(8,128)S(1)} all-gather(f32[128,5]{0,1:T(8,128)S(1)} %get-tuple-element.1071), channel_id=1, replica_groups=mesh['blk'=32,'head'=4] {'blk'}, dimensions={0}, use_global_device_ids=true | all-gather | bytes 84480 | tf_op jit(solution)/shard_map/all_gather | solution.py:176
  768.9 106.4 %all_gather.33 = f32[4096,5]{1,0:T(8,128)} all-gather(f32[128,5]{1,0:T(8,128)S(1)} %get-tuple-element.814), channel_id=1, replica_groups=mesh['blk'=32,'head'=4] {'blk'}, dimensions={0}, use_global_device_ids=true | all-gather | bytes 84480 | tf_op jit(solution)/shard_map/all_gather | solution.py:177
  875.2 2.2 copy.175
  878.4 4.8 all-to-all-start
  883.2 28.4 %while.53 = (s32[]{:T(128)}, f32[128,5,128]{0,2,1:T(8,128)S(1)}, bf16[4096,5,128]{2,0,1:T(8,128)(2,1)}, bf16[128,5,128]{2,0,1:T(8,128)(2,1)S(1)}, f32[128,5]{0,1...) while((s32[]{:T(128)}, f32[128,5,128]{0,2,1:T(8,128)S(1)}, ...), condition=%wide.region_7.0_spmd.clone, body=%wide.region_6.0_spmd.clone.sunk | while | flops 253460480 | bytes 5577392 | solution.py:32
  884.6 2.0 fusion.137
  888.2 2.0 fusion.137
  891.7 2.0 fusion.137
  895.3 2.1 fusion.137
  898.9 2.0 fusion.137
  902.4 2.0 fusion.137
  906.0 2.1 fusion.137
  913.1 8.0 copy.169
  921.1 91.7 %all-gather.15.cloned.1.call-done = bf16[4096,640]{0,1:T(8,128)(2,1)} async-done(((bf16[128,640]{0,1:T(8,128)(2,1)}), bf16[4096,640]{0,1:T(8,128)(2,1)}) %all-gather.15.cloned.1.call-update) | async-done | bytes 5242896 | tf_op jit(solution)/shard_map/all_gather | solution.py:184
  1012.8 42.7 %while.54 = (s32[]{:T(128)}, f32[128,5,128]{0,2,1:T(8,128)S(1)}, f32[128,5,128]{0,2,1:T(8,128)S(1)}, bf16[4096,5,128]{0,2,1:T(8,128)(2,1)}, bf16[128,5,128]{2,0,...) while((s32[]{:T(128)}, f32[128,5,128]{0,2,1:T(8,128)S(1)}, ...), condition=%wide.region_9.0_spmd.clone, body=%wide.region_8.0_spmd.clone.sunk | while | flops 337838080 | bytes 8255169 | solution.py:32
  1016.0 2.1 fusion.146
  1021.3 2.1 fusion.146
  1026.7 2.1 fusion.146
  1032.0 2.1 fusion.146
  1037.4 2.1 fusion.146
  1042.7 2.1 fusion.146
  1048.1 2.1 fusion.146
  1053.4 2.1 fusion.146
  (188 shorter events, 127.1 us)
Async XLA Ops:
  7.2 6.3 copy-start.4
  7.2 6.7 copy-start.5
  7.2 147.8 %all-gather.7.cloned.1.call-start = ((), (), s32[]{:S(2)}) async-start(), calls=%async_computation.3 | async-start | bytes 5406720 | tf_op jit(solution)/shard_map/all_gather | solution.py:138
  9.1 297.2 %all-gather.13.cloned.1.call-start = ((), (), s32[]{:S(2)}) async-start(), calls=%async_computation.6 | async-start | bytes 5406720 | tf_op jit(solution)/shard_map/all_gather | solution.py:141
  9.8 453.3 %all-gather.11.cloned.1.call-start = ((), (), s32[]{:S(2)}) async-start(), calls=%async_computation.5 | async-start | bytes 5406720 | tf_op jit(solution)/shard_map/all_gather | solution.py:139
  11.6 598.3 %all-gather.9.cloned.1.call-start = ((), (), s32[]{:S(2)}) async-start(), calls=%async_computation.4 | async-start | bytes 5406720 | tf_op jit(solution)/shard_map/all_gather | solution.py:140
  13.4 899.7 %all-gather.17.cloned.1.call-start = ((), (), s32[]{:S(2)}) async-start(), calls=%async_computation.8 | async-start | bytes 5406720 | tf_op jit(solution)/shard_map/all_gather | solution.py:185
  13.7 149.2 %copy-start = (bf16[128,640]{0,1:T(8,128)(2,1)}, bf16[128,640]{0,1:T(8,128)(2,1)S(1)}, u32[]{:S(2)}) copy-start(bf16[128,640]{0,1:T(8,128)(2,1)S(1)} %copy.146) | copy-start | bytes 491524
  684.4 8.7 copy-start.6
  684.8 18.6 %copy-start.1 = (bf16[128,640]{0,1:T(8,128)(2,1)S(1)}, bf16[128,640]{0,1:T(8,128)(2,1)}, u32[]{:S(2)}) copy-start(bf16[128,640]{0,1:T(8,128)(2,1)} %copy.145) | copy-start | bytes 491524
  685.0 18.5 %copy-start.2 = (bf16[128,640]{0,1:T(8,128)(2,1)S(1)}, bf16[128,640]{0,1:T(8,128)(2,1)}, u32[]{:S(2)}) copy-start(bf16[128,640]{0,1:T(8,128)(2,1)} %copy.149) | copy-start | bytes 491524
  693.1 75.3 %copy-start.3 = (bf16[4,4,8,640]{3,2,0,1:T(8,128)(2,1)}, bf16[4,4,8,640]{3,2,0,1:T(8,128)(2,1)S(1)}, u32[]{:S(2)}) copy-start(bf16[4,4,8,640]{3,2,0,1:T(8,128)(2,1)S(1)} %copy.192) | copy-start | bytes 491524
  702.7 310.1 %all-gather.15.cloned.1.call-start = ((), (), s32[]{:S(2)}) async-start(), calls=%async_computation.7 | async-start | bytes 5406720 | tf_op jit(solution)/shard_map/all_gather | solution.py:184
  878.4 34.1 %all-to-all-start = ((bf16[4,32,640]{2,1,0:T(8,128)(2,1)}), bf16[4,32,640]{2,1,0:T(8,128)(2,1)S(1)}, u32[]{:S(2)}, u32[]{:S(2)}) async-start(bf16[4,32,640]{2,1,0:T(8,128)(2,1)} %all_to_all.42), calls=%async_computation | async-start | bytes 327680 | tf_op jit(solution)/shard_map/all_to_all | solution.py:161
Sparse Core Ops, SparseCore 0:
  10.1 144.7 all-gather.6
  156.6 149.6 all-gather.12
  308.4 154.6 all-gather.10
  465.1 144.7 all-gather.8
  702.8 152.3 all-gather.16
  856.6 156.1 all-gather.14
where the time goes:
time: 1070 us; the launch traced here: 1060 us
  waiting for transfers between devices  673 us (63%)
  blocking collectives  188 us (18%)
  matrix products  142 us (13%)
  local copies, waits for them, and re-layouts  38.6 us (4%)
  between operations  14.4 us (1%)
    all_gather x1, waiting for transfers between devices, per_device(): lax.all_gather(value_vectors, 'blk', axis=0, tiled=True)  149 us
    all_gather x1, waiting for transfers between devices, per_device(): lax.all_gather(tangent_keys, 'blk', axis=0, tiled=True)  147 us
    all_gather x1, waiting for transfers between devices, per_device(): lax.all_gather(tangent_values, 'blk', axis=0, tiled=True)  143 us
    all_gather x1, waiting for transfers between devices, per_device(): lax.all_gather(key_vectors, 'blk', axis=0, tiled=True)  141 us
    all_gather x1, blocking collectives, per_device(): lax.all_gather(inner_sums, 'blk', axis=0, tiled=True)  106 us
    all_gather x1, waiting for transfers between devices, per_device(): lax.all_gather(query_vectors, 'blk', axis=0, tiled=True)  91.7 us
    all_gather x1, blocking collectives, per_device(): lax.all_gather(log_total, 'blk', axis=0, tiled=True)  63.6 us
  transfers between devices with their start and end apart: 7, of which 5 were waited for; matrix products, arithmetic and copies ran while one was open for 6% of the time, Pallas kernels for 0%

commit v1 on v0

--- a/solution.py
+++ b/solution.py
@@ -136,7 +136,9 @@
     extra_start = ()
     shards = (
         lax.all_gather(key_vectors, "blk", axis=0, tiled=True),
-        lax.all_gather(value_vectors, "blk", axis=0, tiled=True),
+        jnp.concatenate(
+            lax.all_to_all(jnp.stack([value_vectors] * lax.axis_size("blk")), "blk", 0, 0), axis=0
+        ),
         lax.all_gather(tangent_keys, "blk", axis=0, tiled=True),
         lax.all_gather(tangent_values, "blk", axis=0, tiled=True),
     )

time: 1070 us -> 1020 us (0.953)
  waiting for transfers between devices: 673 us -> 588 us
  local copies, waits for them, and re-layouts: 38.6 us -> 58.4 us
    all_gather x1, waiting for transfers between devices: 149 us -> 0.01 us  [per_device(): lax.all_gather(value_vectors, 'blk', axis=0, tiled=True)]
    all_to_all x0 -> x1, waiting for transfers between devices: none -> 78.4 us  [per_device(): lax.all_to_all(jnp.stack([value_vectors] * lax.axis_size('blk')), 'blk',...]
    all_gather x1, waiting for transfers between devices: 141 us -> 77.8 us  [per_device(): lax.all_gather(key_vectors, 'blk', axis=0, tiled=True)]
    all_gather x1, waiting for transfers between devices: 91.7 us -> 137 us  [per_device(): lax.all_gather(query_vectors, 'blk', axis=0, tiled=True)]
    another operation x0 -> x2, local copies, waits for them, and re-layouts: none -> 12.4 us  [the longest x1 8.86 us: split_heads(): matrix.reshape(matrix.shape[0], head_count, matrix.shape[1] // head_count)]
  transfers between devices with their start and end apart: 7 -> 8, of which waited for: 5 -> 5; matrix products, arithmetic and copies ran while one was open for 6% -> 15% of each run, Pallas kernels for 0% -> 0%
where the time goes in v1:
time: 1020 us
  waiting for transfers between devices  588 us (58%)
  blocking collectives  195 us (19%)
  matrix products  142 us (14%)
  local copies, waits for them, and re-layouts  58.4 us (6%)
  between operations  14.4 us (1%)
  starting transfers between devices  13.7 us (1%)
    all_gather x1, waiting for transfers between devices, per_device(): lax.all_gather(tangent_keys, 'blk', axis=0, tiled=True)  149 us
    all_gather x1, waiting for transfers between devices, per_device(): lax.all_gather(tangent_values, 'blk', axis=0, tiled=True)  144 us
    all_gather x1, waiting for transfers between devices, per_device(): lax.all_gather(query_vectors, 'blk', axis=0, tiled=True)  137 us
    all_gather x1, blocking collectives, per_device(): lax.all_gather(inner_sums, 'blk', axis=0, tiled=True)  113 us
    all_to_all x1, waiting for transfers between devices, per_device(): lax.all_to_all(jnp.stack([value_vectors] * lax.axis_size('blk')), 'blk',...  78.4 us
    all_gather x1, waiting for transfers between devices, per_device(): lax.all_gather(key_vectors, 'blk', axis=0, tiled=True)  77.8 us
    all_gather x1, blocking collectives, per_device(): lax.all_gather(log_total, 'blk', axis=0, tiled=True)  64.6 us
  transfers between devices with their start and end apart: 8, of which 5 were waited for; matrix products, arithmetic and copies ran while one was open for 15% of the time, Pallas kernels for 0%

profile of v1, /device:TPU:78, one launch (start us, length us, event | category | flops | bytes accessed | tf_op | source)
XLA Modules:
  0.0 1016.1 jit_solution(18047807967926515273)
XLA Ops:
  12.6 3.6 stack.2
  16.2 8.7 all-to-all-start
  26.2 78.4 %all-to-all-done = bf16[32,128,640]{1,2,0:T(8,128)(2,1)} async-done(((bf16[32,128,640]{1,2,0:T(8,128)(2,1)}), bf16[32,128,640]{1,2,0:T(8,128)(2,1)}, u32[]{:S(2)}, u32[]{:S(2)}) %all-to-all-start) | async-done | bytes 5242912 | tf_op jit(solution)/shard_map/all_to_all | solution.py:140
  104.6 8.2 copy.195
  112.8 8.9 reshape_reshape.3
  121.7 77.8 %all-gather.7.cloned.1.call-done = bf16[4096,640]{0,1:T(8,128)(2,1)} async-done(((bf16[128,640]{0,1:T(8,128)(2,1)}), bf16[4096,640]{0,1:T(8,128)(2,1)}) %all-gather.7.cloned.1.call-update) | async-done | bytes 5242896 | tf_op jit(solution)/shard_map/all_gather | solution.py:138
  199.4 7.8 copy.197
  207.3 144.4 %all-gather.11.cloned.1.call-done = bf16[4096,640]{1,0:T(8,128)(2,1)} async-done(((bf16[128,640]{1,0:T(8,128)(2,1)}), bf16[4096,640]{1,0:T(8,128)(2,1)}) %all-gather.11.cloned.1.call-update) | async-done | bytes 5242896 | tf_op jit(solution)/shard_map/all_gather | solution.py:143
  351.7 7.9 copy.196
  359.6 148.9 %all-gather.9.cloned.1.call-done = bf16[4096,640]{0,1:T(8,128)(2,1)} async-done(((bf16[128,640]{0,1:T(8,128)(2,1)}), bf16[4096,640]{0,1:T(8,128)(2,1)}) %all-gather.9.cloned.1.call-update) | async-done | bytes 5242896 | tf_op jit(solution)/shard_map/all_gather | solution.py:142
  508.5 74.0 %while.52 = (s32[]{:T(128)}, f32[128,5]{0,1:T(8,128)S(1)}, f32[128,5]{0,1:T(8,128)S(1)}, f32[128,5]{0,1:T(8,128)S(1)}, f32[128,5,128]{0,2,1:T(8,128)S(1)}, /*ind...) while((s32[]{:T(128)}, f32[128,5]{0,1:T(8,128)S(1)}, ...), condition=%wide.region_4.0_spmd.clone, body=%wide.region_0.0_spmd.clone.sunk | while | flops 508481920 | bytes 16937192 | solution.py:32
  583.8 8.1 all_to_all.62
  592.0 9.5 all_to_all.63
  602.5 64.6 %all_gather.30 = f32[4096,5]{0,1:T(8,128)S(1)} all-gather(f32[128,5]{0,1:T(8,128)S(1)} %get-tuple-element.1105), channel_id=1, replica_groups=mesh['blk'=32,'head'=4] {'blk'}, dimensions={0}, use_global_device_ids=true | all-gather | bytes 84480 | tf_op jit(solution)/shard_map/all_gather | solution.py:178
  668.7 112.7 %all_gather.32 = f32[4096,5]{1,0:T(8,128)} all-gather(f32[128,5]{1,0:T(8,128)S(1)} %get-tuple-element.848), channel_id=1, replica_groups=mesh['blk'=32,'head'=4] {'blk'}, dimensions={0}, use_global_device_ids=true | all-gather | bytes 84480 | tf_op jit(solution)/shard_map/all_gather | solution.py:179
  781.4 2.2 copy.222
  784.5 4.8 all-to-all-start.1
  789.3 28.6 %while.53 = (s32[]{:T(128)}, f32[128,5,128]{0,2,1:T(8,128)S(1)}, bf16[4096,5,128]{2,0,1:T(8,128)(2,1)}, bf16[128,5,128]{2,0,1:T(8,128)(2,1)S(1)}, f32[128,5]{0,1...) while((s32[]{:T(128)}, f32[128,5,128]{0,2,1:T(8,128)S(1)}, ...), condition=%wide.region_7.0_spmd.clone, body=%wide.region_6.0_spmd.clone.sunk | while | flops 253460480 | bytes 5577392 | solution.py:32
  790.8 2.1 fusion.137
  794.4 2.1 fusion.137
  801.6 2.1 fusion.137
  819.5 8.0 copy.216
  827.5 137.3 %all-gather.15.cloned.1.call-done = bf16[4096,640]{0,1:T(8,128)(2,1)} async-done(((bf16[128,640]{0,1:T(8,128)(2,1)}), bf16[4096,640]{0,1:T(8,128)(2,1)}) %all-gather.15.cloned.1.call-update) | async-done | bytes 5242896 | tf_op jit(solution)/shard_map/all_gather | solution.py:186
  964.7 42.8 %while.54 = (s32[]{:T(128)}, f32[128,5,128]{0,2,1:T(8,128)S(1)}, f32[128,5,128]{0,2,1:T(8,128)S(1)}, bf16[4096,5,128]{0,2,1:T(8,128)(2,1)}, bf16[128,5,128]{2,0,...) while((s32[]{:T(128)}, f32[128,5,128]{0,2,1:T(8,128)S(1)}, ...), condition=%wide.region_9.0_spmd.clone, body=%wide.region_8.0_spmd.clone.sunk | while | flops 337838080 | bytes 8255169 | solution.py:32
  967.9 2.1 fusion.146
  973.3 2.1 fusion.146
  978.6 2.1 fusion.146
  984.0 2.1 fusion.146
  989.3 2.1 fusion.146
  994.7 2.1 fusion.146
  1000.0 2.1 fusion.146
  1005.4 2.1 fusion.146
  (195 shorter events, 135.2 us)
Async XLA Ops:
  7.2 192.3 %all-gather.7.cloned.1.call-start = ((), (), s32[]{:S(2)}) async-start(), calls=%async_computation.4 | async-start | bytes 5406720 | tf_op jit(solution)/shard_map/all_gather | solution.py:138
  9.0 342.7 %all-gather.11.cloned.1.call-start = ((), (), s32[]{:S(2)}) async-start(), calls=%async_computation.6 | async-start | bytes 5406720 | tf_op jit(solution)/shard_map/all_gather | solution.py:143
  9.7 498.8 %all-gather.9.cloned.1.call-start = ((), (), s32[]{:S(2)}) async-start(), calls=%async_computation.5 | async-start | bytes 5406720 | tf_op jit(solution)/shard_map/all_gather | solution.py:142
  12.6 3.6 copy-start
  16.2 9.4 copy-start.5
  16.2 9.7 copy-start.6
  16.2 88.5 %all-to-all-start = ((bf16[32,128,640]{1,2,0:T(8,128)(2,1)}), bf16[32,128,640]{1,2,0:T(8,128)(2,1)}, u32[]{:S(2)}, u32[]{:S(2)}) async-start(bf16[32,128,640]{1,2,0:T(8,128)(2,1)} %stack.2), calls=%async_computation | async-start | bytes 10485760 | tf_op jit(solution)/shard_map/all_to_all | solution.py:140
  24.9 764.5 %all-gather.13.cloned.1.call-start = ((), (), s32[]{:S(2)}) async-start(), calls=%async_computation.7 | async-start | bytes 5406720 | tf_op jit(solution)/shard_map/all_gather | solution.py:185
  25.4 794.0 %all-gather.17.cloned.1.call-start = ((), (), s32[]{:S(2)}) async-start(), calls=%async_computation.9 | async-start | bytes 5406720 | tf_op jit(solution)/shard_map/all_gather | solution.py:187
  25.7 87.1 %copy-start.2 = (bf16[128,640]{0,1:T(8,128)(2,1)}, bf16[128,640]{0,1:T(8,128)(2,1)S(1)}, u32[]{:S(2)}) copy-start(bf16[128,640]{0,1:T(8,128)(2,1)S(1)} %copy.191) | copy-start | bytes 491524
  583.2 8.7 copy-start.7
  583.6 18.6 %copy-start.1 = (bf16[128,640]{0,1:T(8,128)(2,1)S(1)}, bf16[128,640]{0,1:T(8,128)(2,1)}, u32[]{:S(2)}) copy-start(bf16[128,640]{0,1:T(8,128)(2,1)} %copy-done) | copy-start | bytes 491524
  583.8 18.5 %copy-start.3 = (bf16[128,640]{0,1:T(8,128)(2,1)S(1)}, bf16[128,640]{0,1:T(8,128)(2,1)}, u32[]{:S(2)}) copy-start(bf16[128,640]{0,1:T(8,128)(2,1)} %copy.190) | copy-start | bytes 491524
  591.9 76.4 %copy-start.4 = (bf16[4,4,8,640]{3,2,0,1:T(8,128)(2,1)}, bf16[4,4,8,640]{3,2,0,1:T(8,128)(2,1)S(1)}, u32[]{:S(2)}) copy-start(bf16[4,4,8,640]{3,2,0,1:T(8,128)(2,1)S(1)} %copy.239) | copy-start | bytes 491524
  601.5 363.2 %all-gather.15.cloned.1.call-start = ((), (), s32[]{:S(2)}) async-start(), calls=%async_computation.8 | async-start | bytes 5406720 | tf_op jit(solution)/shard_map/all_gather | solution.py:186
  784.5 34.3 %all-to-all-start.1 = ((bf16[4,32,640]{2,1,0:T(8,128)(2,1)}), bf16[4,32,640]{2,1,0:T(8,128)(2,1)S(1)}, u32[]{:S(2)}, u32[]{:S(2)}) async-start(bf16[4,32,640]{2,1,0:T(8,128)(2,1)} %all_to_all.46), calls=%async_computation.1 | async-start | bytes 327680 | tf_op jit(solution)/shard_map/all_to_all | solution.py:163
Sparse Core Ops, SparseCore 0:
  10.1 189.2 all-gather.6
  201.1 150.5 all-gather.10
  353.8 154.6 all-gather.8
  510.5 145.3 all-gather.12
  657.4 151.8 all-gather.16
  810.8 153.9 all-gather.14
